TPU v7x, 32 devices: a whole 2x2x4 slice. The times are simulated.
32 devices in a mesh: narrow: 4 (over y, x), wide: 8 (over z, core).
Axes of the slice: x: 2, y: 2, z: 4, core: 2. Of those that a mesh axis runs over, the one named last changes fastest.
Arguments:
- inputs_one: bfloat16 [32, 1024, 512], P(('narrow', 'wide')), may hold values from -6 to 6
- inputs_two: bfloat16 [32, 1024, 512], P(('narrow', 'wide')), may hold values from -6 to 6
- memory: bfloat16 [32, 1024, 512], P(('narrow', 'wide')), may hold values from -6 to 6
- cotangent_one: bfloat16 [32, 1024, 512], P(('narrow', 'wide')), may hold values from -6 to 6
- cotangent_two: bfloat16 [32, 1024, 512], P(('narrow', 'wide')), may hold values from -6 to 6
- target_ids: int32 [32, 1024], P(('narrow', 'wide')), may hold values from -1 to 3, as said below
- memory_ids: int32 [32, 1024], P(('narrow', 'wide')), may hold values from -1 to 3, as said below
- norm_gain: bfloat16 [3, 512], P(None, 'wide'), may hold values from 0.5 to 1.5
- norm_shift: bfloat16 [3, 512], P(None, 'wide'), may hold values from -1.796875 to 1.796875
- self_qkv: bfloat16 [512, 1536], P('wide'), may hold values from -0.25 to 0.25
- self_out: bfloat16 [512, 512], P('wide'), may hold values from -1 to 1
- cross_query: bfloat16 [512, 512], P('wide'), may hold values from -0.25 to 0.25
- cross_kv: bfloat16 [512, 1024], P('wide'), may hold values from -0.25 to 0.25
- cross_out: bfloat16 [512, 512], P('wide'), may hold values from -1 to 1
- ffn_in: bfloat16 [512, 2048], P('wide'), may hold values from -0.25 to 0.25
- ffn_out: bfloat16 [2048, 512], P('wide'), may hold values from -0.125 to 0.125
Outputs:
- out_one: bfloat16 [32, 1024, 512], P(('narrow', 'wide'))
- out_two: bfloat16 [32, 1024, 512], P(('narrow', 'wide'))
- grad_in_one: float32 [32, 1024, 512], P(('narrow', 'wide'))
- grad_in_two: float32 [32, 1024, 512], P(('narrow', 'wide'))
- grad_memory: float32 [32, 1024, 512], P(('narrow', 'wide'))
- grad_norm_gain: float32 [3, 512], P(None, 'wide')
- grad_norm_shift: float32 [3, 512], P(None, 'wide')
- grad_self_qkv: float32 [512, 1536], P('wide')
- grad_self_out: float32 [512, 512], P('wide')
- grad_cross_query: float32 [512, 512], P('wide')
- grad_cross_kv: float32 [512, 1024], P('wide')
- grad_cross_out: float32 [512, 512], P('wide')
- grad_ffn_in: float32 [512, 2048], P('wide')
- grad_ffn_out: float32 [2048, 512], P('wide')
Inputs may be any that keep to these rules, and one draw needn't show every extreme that they name: `target_ids`: in every row, the ids are 0 to 3 in increasing order, each document one or more slots, followed by one or more padding slots of id -1; every id from -1 to 3 occurs in every row. `memory_ids`: in every row, the ids are 0 to 3 in increasing order, each document one or more slots, followed by one or more padding slots of id -1; every id from -1 to 3 occurs in every row.
All inputs are finite; a program needn't handle non-finite values.
Results may differ from a plain program's by a relative error of at most 0.023.
Values may be sent and summed in bfloat16 or wider, within the bound.
A program may use at most 256 MiB of HBM per device.

v0:
```python
import jax
import jax.numpy as jnp
from jax import lax
from jax.sharding import PartitionSpec as P

HEAD_DIM = 64


def norm_forward(values, gain, shift):
    centre = jnp.mean(values, -1, keepdims=True)
    centred = values - centre
    spread = jnp.mean(centred * centred, -1, keepdims=True)
    return centred * lax.rsqrt(spread + 1e-05) * gain + shift


def norm_backward(values, gain, shift, incoming):
    _, pull = jax.vjp(norm_forward, values, gain, shift)
    return pull(incoming)


def smooth_gate(values):
    return jax.nn.gelu(values, approximate=True)


def gate_backward(values, incoming):
    _, pull = jax.vjp(smooth_gate, values)
    return pull(incoming)[0]


def lower(values):
    return values.astype(jnp.bfloat16)


def project(left, weight):
    return jnp.dot(left, weight, preferred_element_type=jnp.float32)


def project_back(grad_rows, weight):
    return jnp.einsum("no,io->ni", grad_rows, weight, preferred_element_type=jnp.float32)


def outer_grad(left, grad_rows):
    return jnp.einsum("ni,no->io", left, grad_rows, preferred_element_type=jnp.float32)


def blocks_of(tensor, block_rows):
    dims_of = tensor.shape
    moved = tensor.reshape((dims_of[0], dims_of[1] // block_rows, block_rows) + dims_of[2:])
    return jnp.moveaxis(moved, 1, 0)


def unblock(tensor):
    moved = jnp.moveaxis(tensor, 0, 1)
    dims_of = moved.shape
    return moved.reshape((dims_of[0], dims_of[1] * dims_of[2]) + dims_of[3:])


def masked_scores(query_block, keys, query_ids, key_ids):
    scores = jnp.einsum("sqhe,skhe->shqk", query_block, keys, preferred_element_type=jnp.float32)
    scores = scores * query_block.shape[-1] ** (-0.5)
    allowed = (query_ids[:, :, None] == key_ids[:, None, :])[:, None]
    return jnp.where(allowed, scores, -1e30)


def attend_forward(query, keys, values, query_ids, key_ids):
    block_rows = min(512, query.shape[1])

    def one_block(pieces):
        query_block, ids_block = pieces
        scores = masked_scores(query_block, keys, ids_block, key_ids)
        highest = jnp.max(scores, -1, keepdims=True)
        expon = jnp.exp(scores - highest)
        denominator = jnp.sum(expon, -1, keepdims=True)
        probabilities = lower(expon / denominator)
        result = jnp.einsum(
            "shqk,skhe->sqhe", probabilities, values, preferred_element_type=jnp.float32
        )
        return (result, (highest + jnp.log(denominator))[..., 0])

    result, log_total = lax.map(
        one_block, (blocks_of(query, block_rows), blocks_of(query_ids, block_rows))
    )
    return (unblock(result), log_total)


def attend_backward(query, keys, values, query_ids, key_ids, log_total, grad_out):
    block_rows = min(512, query.shape[1])
    scale = query.shape[-1] ** (-0.5)

    def one_block(running, pieces):
        query_block, ids_block, total_block, grad_block = pieces
        scores = masked_scores(query_block, keys, ids_block, key_ids)
        probabilities = jnp.exp(scores - total_block[..., None])
        grad_probs = jnp.einsum(
            "sqhe,skhe->shqk", grad_block, values, preferred_element_type=jnp.float32
        )
        centre = jnp.sum(probabilities * grad_probs, -1, keepdims=True)
        grad_scores = lower(probabilities * (grad_probs - centre))
        grad_query = (
            jnp.einsum("shqk,skhe->sqhe", grad_scores, keys, preferred_element_type=jnp.float32)
            * scale
        )
        grad_keys = (
            running[0]
            + jnp.einsum(
                "shqk,sqhe->skhe", grad_scores, query_block, preferred_element_type=jnp.float32
            )
            * scale
        )
        grad_values = running[1] + jnp.einsum(
            "shqk,sqhe->skhe", lower(probabilities), grad_block, preferred_element_type=jnp.float32
        )
        return ((grad_keys, grad_values), grad_query)

    zeros_kv = jnp.zeros(keys.shape, jnp.float32)
    (grad_keys, grad_values), grad_query = lax.scan(
        one_block,
        (zeros_kv, zeros_kv),
        (
            blocks_of(query, block_rows),
            blocks_of(query_ids, block_rows),
            log_total,
            blocks_of(grad_out, block_rows),
        ),
    )
    return (unblock(grad_query), grad_keys, grad_values)


def to_heads(tensor, row_count, length):
    return tensor.reshape(row_count, length, tensor.shape[-1] // HEAD_DIM, HEAD_DIM)


def step_forward(inputs, kv_cross, target_ids, memory_ids, weights):
    gain, shift, w_qkv, w_self, w_query, w_kv, w_cross, w_in, w_out = weights
    gain_f32 = gain.astype(jnp.float32)
    shift_f32 = shift.astype(jnp.float32)
    row_count, length, model_width = inputs.shape
    flat_in = inputs.astype(jnp.float32).reshape(row_count * length, model_width)
    normed = lower(norm_forward(flat_in, gain_f32[0], shift_f32[0]))
    joined = lower(project(normed, w_qkv))
    query = to_heads(joined[:, :model_width], row_count, length)
    keys = to_heads(joined[:, model_width : 2 * model_width], row_count, length)
    values = to_heads(joined[:, 2 * model_width :], row_count, length)
    attended, log_self = attend_forward(query, keys, values, target_ids, target_ids)
    mixed = lower(attended.reshape(-1, model_width))
    after_self = flat_in + project(mixed, w_self)
    normed_two = lower(norm_forward(after_self, gain_f32[1], shift_f32[1]))
    asked = lower(project(normed_two, w_query))
    mem_keys = to_heads(kv_cross[:, :model_width], row_count, length)
    mem_values = to_heads(kv_cross[:, model_width:], row_count, length)
    fetched, log_cross = attend_forward(
        to_heads(asked, row_count, length), mem_keys, mem_values, target_ids, memory_ids
    )
    fetched = lower(fetched.reshape(-1, model_width))
    after_cross = after_self + project(fetched, w_cross)
    normed_three = lower(norm_forward(after_cross, gain_f32[2], shift_f32[2]))
    preact = project(normed_three, w_in)
    hidden = lower(smooth_gate(preact))
    result = after_cross + project(hidden, w_out)
    saved_state = (
        flat_in,
        normed,
        joined,
        log_self,
        mixed,
        after_self,
        normed_two,
        asked,
        log_cross,
        fetched,
        after_cross,
        normed_three,
        preact,
        hidden,
    )
    return (result.reshape(inputs.shape).astype(jnp.bfloat16), saved_state)


def step_backward(cotangent, saved_state, kv_cross, target_ids, memory_ids, weights):
    gain, shift, w_qkv, w_self, w_query, w_kv, w_cross, w_in, w_out = weights
    gain_f32 = gain.astype(jnp.float32)
    shift_f32 = shift.astype(jnp.float32)
    (
        flat_in,
        normed,
        joined,
        log_self,
        mixed,
        after_self,
        normed_two,
        asked,
        log_cross,
        fetched,
        after_cross,
        normed_three,
        preact,
        hidden,
    ) = saved_state
    row_count, length, model_width = cotangent.shape
    grad_out = cotangent.astype(jnp.float32).reshape(-1, model_width)
    grad_low = lower(grad_out)
    grad_w_out = outer_grad(hidden, grad_low)
    grad_pre = lower(gate_backward(preact, project_back(grad_low, w_out)))
    grad_w_in = outer_grad(normed_three, grad_pre)
    grad_norm3, gain_three, shift_three = norm_backward(
        after_cross, gain_f32[2], shift_f32[2], project_back(grad_pre, w_in)
    )
    grad_cross_in = grad_out + grad_norm3
    cross_low = lower(grad_cross_in)
    grad_w_cross = outer_grad(fetched, cross_low)
    grad_fetched = lower(project_back(cross_low, w_cross))
    mem_keys = to_heads(kv_cross[:, :model_width], row_count, length)
    mem_values = to_heads(kv_cross[:, model_width:], row_count, length)
    grad_asked, grad_mem_keys, grad_mem_values = attend_backward(
        to_heads(asked, row_count, length),
        mem_keys,
        mem_values,
        target_ids,
        memory_ids,
        log_cross,
        to_heads(grad_fetched, row_count, length),
    )
    grad_asked = lower(grad_asked.reshape(-1, model_width))
    grad_w_query = outer_grad(normed_two, grad_asked)
    grad_norm2, gain_two, shift_two = norm_backward(
        after_self, gain_f32[1], shift_f32[1], project_back(grad_asked, w_query)
    )
    grad_self_in = grad_cross_in + grad_norm2
    self_low = lower(grad_self_in)
    grad_w_self = outer_grad(mixed, self_low)
    grad_mixed = lower(project_back(self_low, w_self))
    query = to_heads(joined[:, :model_width], row_count, length)
    keys = to_heads(joined[:, model_width : 2 * model_width], row_count, length)
    values = to_heads(joined[:, 2 * model_width :], row_count, length)
    grad_query, grad_keys, grad_values = attend_backward(
        query,
        keys,
        values,
        target_ids,
        target_ids,
        log_self,
        to_heads(grad_mixed, row_count, length),
    )
    grad_joined = lower(
        jnp.concatenate(
            [
                grad_query.reshape(-1, model_width),
                grad_keys.reshape(-1, model_width),
                grad_values.reshape(-1, model_width),
            ],
            axis=1,
        )
    )
    grad_w_qkv = outer_grad(normed, grad_joined)
    grad_norm1, gain_one, shift_one = norm_backward(
        flat_in, gain_f32[0], shift_f32[0], project_back(grad_joined, w_qkv)
    )
    grad_inputs = (grad_self_in + grad_norm1).reshape(cotangent.shape)
    grad_pair = jnp.concatenate(
        [grad_mem_keys.reshape(-1, model_width), grad_mem_values.reshape(-1, model_width)], axis=1
    )
    parts_grad = (
        jnp.stack([gain_one, gain_two, gain_three]),
        jnp.stack([shift_one, shift_two, shift_three]),
        grad_w_qkv,
        grad_w_self,
        grad_w_query,
        grad_w_cross,
        grad_w_in,
        grad_w_out,
    )
    return (grad_inputs, grad_pair, parts_grad)


def body(
    inputs_one,
    inputs_two,
    memory,
    cotangent_one,
    cotangent_two,
    target_ids,
    memory_ids,
    norm_gain,
    norm_shift,
    self_qkv,
    self_out,
    cross_query,
    cross_kv,
    cross_out,
    ffn_in,
    ffn_out,
):
    owned_parts = (
        norm_gain,
        norm_shift,
        self_qkv,
        self_out,
        cross_query,
        cross_kv,
        cross_out,
        ffn_in,
        ffn_out,
    )

    def collect():
        return (
            lax.all_gather(owned_parts[0], "wide", axis=1, tiled=True),
            lax.all_gather(owned_parts[1], "wide", axis=1, tiled=True),
            lax.all_gather(owned_parts[2], "wide", axis=0, tiled=True),
            lax.all_gather(owned_parts[3], "wide", axis=0, tiled=True),
            lax.all_gather(owned_parts[4], "wide", axis=0, tiled=True),
            lax.all_gather(owned_parts[5], "wide", axis=0, tiled=True),
            lax.all_gather(owned_parts[6], "wide", axis=0, tiled=True),
            lax.all_gather(owned_parts[7], "wide", axis=0, tiled=True),
            lax.all_gather(owned_parts[8], "wide", axis=0, tiled=True),
        )

    current = collect()
    model_width = memory.shape[2]
    flat_memory = memory.reshape(-1, model_width)
    kv_cross = lower(project(flat_memory, current[5]))
    out_one, saved_one = step_forward(inputs_one, kv_cross, target_ids, memory_ids, current)
    current = collect()
    out_two, saved_two = step_forward(inputs_two, kv_cross, target_ids, memory_ids, current)
    current = collect()
    grad_two, pair_two, parts_two = step_backward(
        cotangent_two, saved_two, kv_cross, target_ids, memory_ids, current
    )
    current = collect()
    grad_one, pair_one, parts_one = step_backward(
        cotangent_one, saved_one, kv_cross, target_ids, memory_ids, current
    )
    grad_pair = lower(pair_one + pair_two)
    grad_w_kv = outer_grad(flat_memory, grad_pair)
    grad_memory = project_back(grad_pair, current[5]).reshape(memory.shape)
    whole_grads = (
        parts_one[0] + parts_two[0],
        parts_one[1] + parts_two[1],
        parts_one[2] + parts_two[2],
        parts_one[3] + parts_two[3],
        parts_one[4] + parts_two[4],
        grad_w_kv,
        parts_one[5] + parts_two[5],
        parts_one[6] + parts_two[6],
        parts_one[7] + parts_two[7],
    )
    shares = (
        lax.psum_scatter(
            whole_grads[0].astype(jnp.bfloat16), "wide", scatter_dimension=1, tiled=True
        ).astype(jnp.float32),
        lax.psum_scatter(
            whole_grads[1].astype(jnp.bfloat16), "wide", scatter_dimension=1, tiled=True
        ).astype(jnp.float32),
        lax.psum_scatter(
            whole_grads[2].astype(jnp.bfloat16), "wide", scatter_dimension=0, tiled=True
        ).astype(jnp.float32),
        lax.psum_scatter(
            whole_grads[3].astype(jnp.bfloat16), "wide", scatter_dimension=0, tiled=True
        ).astype(jnp.float32),
        lax.psum_scatter(
            whole_grads[4].astype(jnp.bfloat16), "wide", scatter_dimension=0, tiled=True
        ).astype(jnp.float32),
        lax.psum_scatter(
            whole_grads[5].astype(jnp.bfloat16), "wide", scatter_dimension=0, tiled=True
        ).astype(jnp.float32),
        lax.psum_scatter(
            whole_grads[6].astype(jnp.bfloat16), "wide", scatter_dimension=0, tiled=True
        ).astype(jnp.float32),
        lax.psum_scatter(
            whole_grads[7].astype(jnp.bfloat16), "wide", scatter_dimension=0, tiled=True
        ).astype(jnp.float32),
        lax.psum_scatter(
            whole_grads[8].astype(jnp.bfloat16), "wide", scatter_dimension=0, tiled=True
        ).astype(jnp.float32),
    )
    totals = (
        lax.psum(shares[0].astype(jnp.bfloat16), "narrow").astype(jnp.float32),
        lax.psum(shares[1].astype(jnp.bfloat16), "narrow").astype(jnp.float32),
        lax.psum(shares[2].astype(jnp.bfloat16), "narrow").astype(jnp.float32),
        lax.psum(shares[3].astype(jnp.bfloat16), "narrow").astype(jnp.float32),
        lax.psum(shares[4].astype(jnp.bfloat16), "narrow").astype(jnp.float32),
        lax.psum(shares[5].astype(jnp.bfloat16), "narrow").astype(jnp.float32),
        lax.psum(shares[6].astype(jnp.bfloat16), "narrow").astype(jnp.float32),
        lax.psum(shares[7].astype(jnp.bfloat16), "narrow").astype(jnp.float32),
        lax.psum(shares[8].astype(jnp.bfloat16), "narrow").astype(jnp.float32),
    )
    return (
        out_one,
        out_two,
        grad_one,
        grad_two,
        grad_memory,
        totals[0],
        totals[1],
        totals[2],
        totals[3],
        totals[4],
        totals[5],
        totals[6],
        totals[7],
        totals[8],
    )


def solution(mesh):
    return jax.shard_map(
        body,
        mesh=mesh,
        in_specs=(
            P(("narrow", "wide"), None, None),
            P(("narrow", "wide"), None, None),
            P(("narrow", "wide"), None, None),
            P(("narrow", "wide"), None, None),
            P(("narrow", "wide"), None, None),
            P(("narrow", "wide"), None),
            P(("narrow", "wide"), None),
            P(None, "wide"),
            P(None, "wide"),
            P("wide", None),
            P("wide", None),
            P("wide", None),
            P("wide", None),
            P("wide", None),
            P("wide", None),
            P("wide", None),
        ),
        out_specs=(
            P(("narrow", "wide"), None, None),
            P(("narrow", "wide"), None, None),
            P(("narrow", "wide"), None, None),
            P(("narrow", "wide"), None, None),
            P(("narrow", "wide"), None, None),
            P(None, "wide"),
            P(None, "wide"),
            P("wide", None),
            P("wide", None),
            P("wide", None),
            P("wide", None),
            P("wide", None),
            P("wide", None),
            P("wide", None),
        ),
        check_vma=False,
    )
```

profile of v0, /device:TPU:0, one launch (start us, length us, event | category | flops | bytes accessed | tf_op | source)
XLA Modules:
  0.0 1072.0 jit_solution(11442335120683196524)
XLA Ops:
  10.1 13.7 %all-gather = bf16[8,64,3]{1,2,0:T(4,128)(2,1)S(1)} all-gather(bf16[1,64,3]{1,2,0:T(4,128)(2,1)} %bitcast.837), channel_id=1, replica_groups=mesh['narrow'=4,'wide'=8] {'wide'}, dimensions={0}, use_global_device_ids=true | all-gather | bytes 3456 | tf_op jit(solution)/shard_map/all_gather | solution.py:307
  24.5 8.9 all-gather.1
  34.1 16.9 %all_gather.21 = bf16[512,512]{1,0:T(8,128)(2,1)} all-gather(bf16[64,512]{1,0:T(8,128)(2,1)} %param.42), channel_id=1, replica_groups=mesh['narrow'=4,'wide'=8] {'wide'}, dimensions={0}, use_global_device_ids=true | all-gather | bytes 589824 | tf_op jit(solution)/shard_map/all_gather | solution.py:310
  51.1 17.8 %all_gather.22 = bf16[512,512]{1,0:T(8,128)(2,1)} all-gather(bf16[64,512]{1,0:T(8,128)(2,1)} %param.43), channel_id=1, replica_groups=mesh['narrow'=4,'wide'=8] {'wide'}, dimensions={0}, use_global_device_ids=true | all-gather | bytes 589824 | tf_op jit(solution)/shard_map/all_gather | solution.py:311
  68.9 17.5 %all_gather.24 = bf16[512,512]{1,0:T(8,128)(2,1)} all-gather(bf16[64,512]{1,0:T(8,128)(2,1)S(1)} %copy-done.152), channel_id=1, replica_groups=mesh['narrow'=4,'wide'=8] {'wide'}, dimensions={0}, use_global_device_ids=true | all-gather | bytes 589824 | tf_op jit(solution)/shard_map/all_gather | solution.py:313
  113.7 30.4 %while.110 = (s32[]{:T(128)}, bf16[2,1,512,8,64]{2,4,3,1,0:T(8,128)(2,1)}, f32[2,1,8,512]{3,2,1,0:T(8,128)S(1)}, s32[2,1,512]{2,1,0:T(1,128)S(1)}, s32[1,1024]{1...) while((s32[]{:T(128)}, ...), condition=%wide.region_19.20_spmd, body=%wide.region_16.19_spmd.sunk | while | flops 1124593664 | bytes 64628908 | solution.py:80
  158.2 30.6 %while.111 = (s32[]{:T(128)}, bf16[2,1,512,8,64]{2,4,3,1,0:T(8,128)(2,1)}, f32[2,1,8,512]{3,2,1,0:T(8,128)}, s32[2,1,512]{2,1,0:T(1,128)S(1)}, s32[1,1024]{1,0:T...) while((s32[]{:T(128)}, ...), condition=%wide.region_25.26_spmd, body=%wide.region_22.25_spmd.sunk | while | flops 1124593664 | bytes 64628908 | solution.py:80
  204.4 30.3 %while.108 = (s32[]{:T(128)}, bf16[2,1,512,8,64]{2,4,3,1,0:T(8,128)(2,1)}, f32[2,1,8,512]{3,2,1,0:T(8,128)S(1)}, s32[2,1,512]{2,1,0:T(1,128)S(1)}, s32[1,1024]{1...) while((s32[]{:T(128)}, ...), condition=%wide.region_5.6_spmd, body=%wide.region_2.5_spmd.sunk | while | flops 1124593664 | bytes 64628908 | solution.py:80
  248.3 29.7 %while.109 = (s32[]{:T(128)}, bf16[2,1,512,8,64]{2,4,3,1,0:T(8,128)(2,1)}, f32[2,1,8,512]{3,2,1,0:T(8,128)}, s32[2,1,512]{2,1,0:T(1,128)S(1)}, s32[1,1024]{1,0:T...) while((s32[]{:T(128)}, ...), condition=%wide.region_11.12_spmd, body=%wide.region_8.11_spmd.sunk | while | flops 1124593664 | bytes 64628908 | solution.py:80
  288.7 8.1 fusion.226
  296.9 9.9 fusion.146
  355.6 86.0 %while.114 = (s32[]{:T(128)}, f32[1,1024,8,64]{1,3,2,0:T(8,128)}, f32[1,1024,8,64]{1,3,2,0:T(8,128)}, bf16[2,1,512,8,64]{2,4,3,1,0:T(8,128)(2,1)}, bf16[2,1,512,...) while((s32[]{:T(128)}, f32[1,1024,8,64]{1,3,2,0:T(8,128)}, ...), condition=%wide.region_44.45_spmd.clone, body=%wide.region_42.44_spmd.clone.sunk | while | flops 2725507072 | bytes 217147824 | solution.py:116
  362.3 11.8 %multiply_reduce_fusion.22 = (f32[8,512]{1,0:T(8,128)}, f32[8,512,1024]{2,1,0:T(8,128)}) fusion(f32[8,512,1024]{2,1,0:T(8,128)S(1)} %fusion.405, f32[8,512]{1,0:T(8,128)} %dynamic-slice_bitcast_fusion.10, bf16[1,1024,8,64]{1,3,2,0:T(8,128)(2,1)} %copy-done.7, bf16[2,1,512,8,64]{2,4,3,1,0:T(8,128)(2,1)} %get-tuple-element.1819, s32[]{:T(128)S(6)} %copy.330, ...), kind=kOutput, calls=%fused_computation.135.clone.1 | convolution fusion | flops 557838336 | bytes 35684356 | tf_op jit(solution)/shard_map/while/body/eval_jaxpr/sqhe,skhe->shqk/dot_general | solution.py:59
  374.1 9.4 multiply_convert_fusion.16
  383.6 8.9 bitcast_add_fusion.21
  404.8 11.8 %multiply_reduce_fusion.22 = (f32[8,512]{1,0:T(8,128)}, f32[8,512,1024]{2,1,0:T(8,128)}) fusion(f32[8,512,1024]{2,1,0:T(8,128)S(1)} %fusion.405, f32[8,512]{1,0:T(8,128)} %dynamic-slice_bitcast_fusion.10, bf16[1,1024,8,64]{1,3,2,0:T(8,128)(2,1)} %copy-done.7, bf16[2,1,512,8,64]{2,4,3,1,0:T(8,128)(2,1)} %get-tuple-element.1819, s32[]{:T(128)S(6)} %copy.330, ...), kind=kOutput, calls=%fused_computation.135.clone.1 | convolution fusion | flops 557838336 | bytes 35684356 | tf_op jit(solution)/shard_map/while/body/eval_jaxpr/sqhe,skhe->shqk/dot_general | solution.py:59
  416.6 9.4 multiply_convert_fusion.16
  426.0 9.5 bitcast_add_fusion.21
  453.7 85.9 %while.112 = (s32[]{:T(128)}, f32[1,1024,8,64]{1,3,2,0:T(8,128)}, f32[1,1024,8,64]{1,3,2,0:T(8,128)}, bf16[2,1,512,8,64]{2,4,3,1,0:T(8,128)(2,1)}, bf16[2,1,512,...) while((s32[]{:T(128)}, f32[1,1024,8,64]{1,3,2,0:T(8,128)}, ...), condition=%wide.region_32.33_spmd.clone, body=%wide.region_30.32_spmd.clone.sunk | while | flops 2725507072 | bytes 217147824 | solution.py:116
  459.9 11.8 %multiply_reduce_fusion.20 = (f32[8,512]{1,0:T(8,128)}, f32[8,512,1024]{2,1,0:T(8,128)}) fusion(f32[8,512,1024]{2,1,0:T(8,128)S(1)} %fusion.385, f32[8,512]{1,0:T(8,128)} %dynamic-slice_bitcast_fusion.8, bf16[1,1024,8,64]{1,3,2,0:T(8,128)(2,1)} %copy-done.9, bf16[2,1,512,8,64]{2,4,3,1,0:T(8,128)(2,1)} %get-tuple-element.1858, s32[]{:T(128)S(6)} %copy.342, ...), kind=kOutput, calls=%fused_computation.77.clone.1 | convolution fusion | flops 557838336 | bytes 35684356 | tf_op jit(solution)/shard_map/while/body/eval_jaxpr/sqhe,skhe->shqk/dot_general | solution.py:59
  471.7 9.4 multiply_convert_fusion.14
  481.2 8.9 bitcast_add_fusion.17
  502.4 11.8 %multiply_reduce_fusion.20 = (f32[8,512]{1,0:T(8,128)}, f32[8,512,1024]{2,1,0:T(8,128)}) fusion(f32[8,512,1024]{2,1,0:T(8,128)S(1)} %fusion.385, f32[8,512]{1,0:T(8,128)} %dynamic-slice_bitcast_fusion.8, bf16[1,1024,8,64]{1,3,2,0:T(8,128)(2,1)} %copy-done.9, bf16[2,1,512,8,64]{2,4,3,1,0:T(8,128)(2,1)} %get-tuple-element.1858, s32[]{:T(128)S(6)} %copy.342, ...), kind=kOutput, calls=%fused_computation.77.clone.1 | convolution fusion | flops 557838336 | bytes 35684356 | tf_op jit(solution)/shard_map/while/body/eval_jaxpr/sqhe,skhe->shqk/dot_general | solution.py:59
  514.2 9.4 multiply_convert_fusion.14
  523.6 9.5 bitcast_add_fusion.17
  591.0 85.9 %while.113 = (s32[]{:T(128)}, f32[1,1024,8,64]{1,3,2,0:T(8,128)}, f32[1,1024,8,64]{1,3,2,0:T(8,128)}, bf16[2,1,512,8,64]{2,4,3,1,0:T(8,128)(2,1)}, bf16[2,1,512,...) while((s32[]{:T(128)}, f32[1,1024,8,64]{1,3,2,0:T(8,128)}, ...), condition=%wide.region_37.38_spmd.clone, body=%wide.region_35.37_spmd.clone.sunk | while | flops 2725507072 | bytes 212953488 | solution.py:116
  597.5 11.8 %multiply_reduce_fusion.21 = (f32[8,512]{1,0:T(8,128)}, f32[8,512,1024]{2,1,0:T(8,128)}) fusion(f32[8,512,1024]{2,1,0:T(8,128)S(1)} %fusion.395, f32[8,512]{1,0:T(8,128)} %dynamic-slice_bitcast_fusion.9, bf16[1,1024,8,64]{1,3,2,0:T(8,128)(2,1)} %get-tuple-element.1939, bf16[2,1,512,8,64]{2,4,3,1,0:T(8,128)(2,1)} %get-tuple-element.1936, ...), kind=kOutput, calls=%fused_computation.106.clone.1 | convolution fusion | flops 557838336 | bytes 35684356 | tf_op jit(solution)/shard_map/while/body/eval_jaxpr/sqhe,skhe->shqk/dot_general | solution.py:59
  609.2 9.5 multiply_convert_fusion.15
  618.7 8.9 bitcast_add_fusion.19
  640.1 11.8 %multiply_reduce_fusion.21 = (f32[8,512]{1,0:T(8,128)}, f32[8,512,1024]{2,1,0:T(8,128)}) fusion(f32[8,512,1024]{2,1,0:T(8,128)S(1)} %fusion.395, f32[8,512]{1,0:T(8,128)} %dynamic-slice_bitcast_fusion.9, bf16[1,1024,8,64]{1,3,2,0:T(8,128)(2,1)} %get-tuple-element.1939, bf16[2,1,512,8,64]{2,4,3,1,0:T(8,128)(2,1)} %get-tuple-element.1936, ...), kind=kOutput, calls=%fused_computation.106.clone.1 | convolution fusion | flops 557838336 | bytes 35684356 | tf_op jit(solution)/shard_map/while/body/eval_jaxpr/sqhe,skhe->shqk/dot_general | solution.py:59
  651.9 9.4 multiply_convert_fusion.15
  661.3 9.4 bitcast_add_fusion.19
  690.9 86.0 %while.115 = (s32[]{:T(128)}, f32[1,1024,8,64]{1,3,2,0:T(8,128)}, f32[1,1024,8,64]{1,3,2,0:T(8,128)}, bf16[2,1,512,8,64]{2,4,3,1,0:T(8,128)(2,1)}, bf16[2,1,512,...) while((s32[]{:T(128)}, f32[1,1024,8,64]{1,3,2,0:T(8,128)}, ...), condition=%wide.region_49.50_spmd.clone, body=%wide.region_47.49_spmd.clone.sunk | while | flops 2725507072 | bytes 212953488 | solution.py:116
  697.1 11.8 %multiply_reduce_fusion.23 = (f32[8,512]{1,0:T(8,128)}, f32[8,512,1024]{2,1,0:T(8,128)}) fusion(f32[8,512,1024]{2,1,0:T(8,128)S(1)} %fusion.415, f32[8,512]{1,0:T(8,128)} %dynamic-slice_bitcast_fusion.11, bf16[1,1024,8,64]{1,3,2,0:T(8,128)(2,1)} %get-tuple-element.1900, bf16[2,1,512,8,64]{2,4,3,1,0:T(8,128)(2,1)} %get-tuple-element.1897, ...), kind=kOutput, calls=%fused_computation.164.clone.1 | convolution fusion | flops 557838336 | bytes 35684356 | tf_op jit(solution)/shard_map/while/body/eval_jaxpr/sqhe,skhe->shqk/dot_general | solution.py:59
  708.9 9.5 multiply_convert_fusion.17
  718.4 8.9 bitcast_add_fusion.23
  739.6 11.8 %multiply_reduce_fusion.23 = (f32[8,512]{1,0:T(8,128)}, f32[8,512,1024]{2,1,0:T(8,128)}) fusion(f32[8,512,1024]{2,1,0:T(8,128)S(1)} %fusion.415, f32[8,512]{1,0:T(8,128)} %dynamic-slice_bitcast_fusion.11, bf16[1,1024,8,64]{1,3,2,0:T(8,128)(2,1)} %get-tuple-element.1900, bf16[2,1,512,8,64]{2,4,3,1,0:T(8,128)(2,1)} %get-tuple-element.1897, ...), kind=kOutput, calls=%fused_computation.164.clone.1 | convolution fusion | flops 557838336 | bytes 35684356 | tf_op jit(solution)/shard_map/while/body/eval_jaxpr/sqhe,skhe->shqk/dot_general | solution.py:59
  751.4 9.4 multiply_convert_fusion.17
  760.9 9.5 bitcast_add_fusion.23
  807.8 8.5 add_convert_fusion
  850.0 9.3 fusion.183
  859.3 7.9 fusion.184
  869.0 27.2 %reduce-scatter.26.cloned.1.call-done = bf16[256,512]{1,0:T(8,128)(2,1)} async-done(((bf16[2048,512]{1,0:T(8,128)(2,1)}), bf16[256,512]{1,0:T(8,128)(2,1)}) %reduce-scatter.26.cloned.1.call-update) | async-done | bytes 262160 | tf_op jit(solution)/shard_map/reduce_scatter | solution.py:372
  896.1 36.8 %reduce-scatter.24.cloned.1.call-done = bf16[64,2048]{1,0:T(8,128)(2,1)} async-done(((bf16[512,2048]{1,0:T(8,128)(2,1)}), bf16[64,2048]{1,0:T(8,128)(2,1)}) %reduce-scatter.24.cloned.1.call-update) | async-done | bytes 262160 | tf_op jit(solution)/shard_map/reduce_scatter | solution.py:369
  954.0 10.4 reduce-scatter.30.cloned.1.call-done
  965.2 30.4 %reduce-scatter.28.cloned.1.call-done = bf16[64,3]{1,0:T(8,128)(2,1)} async-done(((bf16[512,3]{1,0:T(8,128)(2,1)}), bf16[64,3]{1,0:T(8,128)(2,1)}) %reduce-scatter.28.cloned.1.call-update) | async-done | bytes 400
  996.4 9.9 all-reduce
  1007.5 46.9 %all-reduce.4.cloned.1.call-done = (bf16[64,1024]{0,1:T(8,128)(2,1)}, bf16[64,1536]{1,0:T(8,128)(2,1)}, bf16[64,512]{1,0:T(8,128)(2,1)}, bf16[64,512]{1,0:T(8,12...) async-done(((bf16[64,1024]{0,1:T(8,128)(2,1)}, bf16[64,1536]{1,0:T(8,128)(2,1)}, bf16[64,512]{1,0:T(8,128)(2,1)}, ...) | async-done | bytes 1048592 | tf_op jit(solution)/shard_map/psum | solution.py:382
  (808 shorter events, 528.9 us)
Async XLA Ops:
  7.2 87.1 %copy-start = (bf16[1,1024,512]{2,1,0:T(8,128)(2,1)S(1)}, bf16[1,1024,512]{2,1,0:T(8,128)(2,1)}, u32[]{:S(2)}) copy-start(bf16[1,1024,512]{2,1,0:T(8,128)(2,1)} %param.34) | copy-start | bytes 3145732
  7.2 61.7 %copy-start.152 = (bf16[64,512]{1,0:T(8,128)(2,1)S(1)}, bf16[64,512]{1,0:T(8,128)(2,1)}, u32[]{:S(2)}) copy-start(bf16[64,512]{1,0:T(8,128)(2,1)} %param.45) | copy-start | bytes 196612
  7.2 79.1 %copy-start.121 = (bf16[1,1024,512]{2,1,0:T(8,128)(2,1)S(1)}, bf16[1,1024,512]{2,1,0:T(8,128)(2,1)}, u32[]{:S(2)}) copy-start(bf16[1,1024,512]{2,1,0:T(8,128)(2,1)} %param.32) | copy-start | bytes 3145732
  7.2 87.1 %all-gather.9.cloned.1.call-start = ((), (), s32[]{:S(2)}) async-start(), calls=%async_computation.10 | async-start | bytes 1179648 | tf_op jit(solution)/shard_map/all_gather | solution.py:312
  7.9 90.4 %all-gather.7.cloned.1.call-start = ((), (), s32[]{:S(2)}) async-start(), calls=%async_computation.9 | async-start | bytes 1769472 | tf_op jit(solution)/shard_map/all_gather | solution.py:309
  8.7 280.0 %all-gather.11.cloned.1.call-start = ((), (), s32[]{:S(2)}) async-start(), calls=%async_computation.11 | async-start | bytes 2359296 | tf_op jit(solution)/shard_map/all_gather | solution.py:314
  9.4 287.4 %all-gather.13.cloned.1.call-start = ((), (), s32[]{:S(2)}) async-start(), calls=%async_computation.12 | async-start | bytes 2359296 | tf_op jit(solution)/shard_map/all_gather | solution.py:315
  10.0 857.2 %reduce-scatter.32.cloned.1.call-start = ((), (), s32[]{:S(2)}) async-start(), calls=%async_computation.21 | async-start | bytes 1179648
  24.5 73.8 %copy-start.153 = (f32[1,512]{1,0:T(1,128)}, f32[1,512]{1,0:T(1,128)S(1)}, u32[]{:S(2)}) copy-start(f32[1,512]{1,0:T(1,128)S(1)} %get-tuple-element.1151) | copy-start | bytes 6148
  34.1 64.2 %copy-start.192 = (f32[1,512]{1,0:T(1,128)}, f32[1,512]{1,0:T(1,128)S(1)}, u32[]{:S(2)}) copy-start(f32[1,512]{1,0:T(1,128)S(1)} %get-tuple-element.1154) | copy-start | bytes 6148
  158.2 30.6 %copy-start.138 = (f32[1024]{0:T(1024)S(1)}, f32[1024]{0:T(1024)}, u32[]{:S(2)}) copy-start(f32[1024]{0:T(1024)} %copy-done.137) | copy-start | bytes 12292
  158.2 30.6 %copy-start.154 = (f32[1,512]{1,0:T(1,128)S(1)}, f32[1,512]{1,0:T(1,128)}, u32[]{:S(2)}) copy-start(f32[1,512]{1,0:T(1,128)} %copy-done.153) | copy-start | bytes 6148
  158.2 30.6 %copy-start.177 = (f32[1024]{0:T(1024)S(1)}, f32[1024]{0:T(1024)}, u32[]{:S(2)}) copy-start(f32[1024]{0:T(1024)} %fusion.209) | copy-start | bytes 12292
  158.2 30.6 %copy-start.193 = (f32[1,512]{1,0:T(1,128)S(1)}, f32[1,512]{1,0:T(1,128)}, u32[]{:S(2)}) copy-start(f32[1,512]{1,0:T(1,128)} %copy-done.192) | copy-start | bytes 6148
  283.9 55.1 %copy-start.146 = (f32[1024]{0:T(1024)}, f32[1024]{0:T(1024)S(1)}, u32[]{:S(2)}) copy-start(f32[1024]{0:T(1024)S(1)} %broadcast_multiply_fusion) | copy-start | bytes 12292
  287.1 51.9 %copy-start.148 = (f32[1024]{0:T(1024)}, f32[1024]{0:T(1024)S(1)}, u32[]{:S(2)}) copy-start(f32[1024]{0:T(1024)S(1)} %broadcast_multiply_fusion.3) | copy-start | bytes 12292
  288.6 50.3 %copy-start.156 = (f32[1024]{0:T(1024)}, f32[1024]{0:T(1024)S(1)}, u32[]{:S(2)}) copy-start(f32[1024]{0:T(1024)S(1)} %fusion.214) | copy-start | bytes 12292
  288.7 50.3 %copy-start.158 = (f32[1024]{0:T(1024)}, f32[1024]{0:T(1024)S(1)}, u32[]{:S(2)}) copy-start(f32[1024]{0:T(1024)S(1)} %fusion.211) | copy-start | bytes 12292
  296.9 9.9 copy-start.199
  374.1 9.4 copy-start.51
  416.6 9.4 copy-start.51
  426.0 9.5 copy-start.1
  426.0 9.5 copy-start.8
  426.0 9.8 copy-start.96
  471.7 9.4 copy-start.50
  514.2 9.4 copy-start.50
  523.6 9.5 copy-start.2
  523.6 9.5 copy-start.10
  523.6 9.8 copy-start.98
  552.4 316.5 %reduce-scatter.22.cloned.1.call-start = ((), (), s32[]{:S(2)}) async-start(), calls=%async_computation.16 | async-start | bytes 589824 | tf_op jit(solution)/shard_map/reduce_scatter | solution.py:366
  589.8 279.1 %reduce-scatter.20.cloned.1.call-start = ((), (), s32[]{:S(2)}) async-start(), calls=%async_computation.15 | async-start | bytes 589824 | tf_op jit(solution)/shard_map/reduce_scatter | solution.py:360
  609.2 9.5 copy-start.49
  651.9 9.4 copy-start.49
  661.3 9.5 copy-start.3
  661.3 9.5 copy-start.15
  661.3 9.8 copy-start.100
  689.7 179.2 %reduce-scatter.18.cloned.1.call-start = ((), (), s32[]{:S(2)}) async-start(), calls=%async_computation.14 | async-start | bytes 589824 | tf_op jit(solution)/shard_map/reduce_scatter | solution.py:357
  708.9 9.5 copy-start.48
  760.8 9.5 copy-start.4
  760.8 9.5 copy-start.13
  760.8 9.8 copy-start.93
  794.3 74.6 %reduce-scatter.16.cloned.1.call-start = ((), (), s32[]{:S(2)}) async-start(), calls=%async_computation.13 | async-start | bytes 1769472 | tf_op jit(solution)/shard_map/reduce_scatter | solution.py:354
  801.6 94.5 %reduce-scatter.26.cloned.1.call-start = ((), (), s32[]{:S(2)}) async-start(), calls=%async_computation.18 | async-start | bytes 2359296 | tf_op jit(solution)/shard_map/reduce_scatter | solution.py:372
  816.4 116.5 %reduce-scatter.24.cloned.1.call-start = ((), (), s32[]{:S(2)}) async-start(), calls=%async_computation.17 | async-start | bytes 2359296 | tf_op jit(solution)/shard_map/reduce_scatter | solution.py:369
  826.4 138.0 %reduce-scatter.30.cloned.1.call-start = ((), (), s32[]{:S(2)}) async-start(), calls=%async_computation.20 | async-start | bytes 147456
  848.8 146.8 %reduce-scatter.28.cloned.1.call-start = ((), (), s32[]{:S(2)}) async-start(), calls=%async_computation.19 | async-start | bytes 147456
  849.7 204.7 %all-reduce.4.cloned.1.call-start = ((), (), s32[]{:S(2)}) async-start(), calls=%async_computation.22 | async-start | bytes 2359296 | tf_op jit(solution)/shard_map/psum | solution.py:382
  1054.4 9.8 copy-start.131
  (214 other events, 702.5 us)
Sparse Core Ops, SparseCore 0:
  9.6 24.7 all-gather.8
  36.1 28.4 all-gather.6
  66.2 30.6 all-gather.10
  98.4 28.9 all-gather.12
  552.6 32.2 reduce-scatter.31
  590.0 30.8 reduce-scatter.21
  689.9 30.8 reduce-scatter.19
  794.4 30.7 reduce-scatter.17
  827.7 32.4 reduce-scatter.15
  862.4 33.7 reduce-scatter.25
  898.5 34.3 reduce-scatter.23
  935.7 28.7 reduce-scatter.29
  967.2 28.3 reduce-scatter.27
  1000.4 53.9 all-reduce.3
where the time goes:
time: 1080 us; the launch traced here: 1070 us
  matrix products  449 us (42%)
  other arithmetic  182 us (17%)
  local copies, waits for them, and re-layouts  180 us (17%)
  waiting for transfers between devices  154 us (14%)
  blocking collectives  84.8 us (8%)
  between operations  16.4 us (2%)
    dot_general x16, matrix products, masked_scores(): jnp.einsum('sqhe,skhe->shqk', query_block, keys, preferred_element_type=j...  125 us
    convert_element_type x12, other arithmetic, lower(): return values.astype(jnp.bfloat16)  79.6 us
    dot_general x8, matrix products, one_block(): jnp.einsum('shqk,sqhe->skhe', lower(probabilities), grad_block, preferred...  73.3 us
    unnamed x355, local copies, waits for them, and re-layouts  56.8 us
    dot_general x13, matrix products, project_back(): jnp.einsum('no,io->ni', grad_rows, weight, preferred_element_type=jnp.flo...  53.1 us
    psum x1, waiting for transfers between devices, body(): lax.psum(shares[5].astype(jnp.bfloat16), 'narrow').astype(jnp.float32)  46.9 us
    dot_general x13, matrix products, project(): return jnp.dot(left, weight, preferred_element_type=jnp.float32)  44.7 us
    dot_general x8, matrix products, one_block(): jnp.einsum('shqk,skhe->sqhe', probabilities, values, preferred_element_ty...  44 us
  transfers between devices with their start and end apart: 14, of which 5 were waited for; matrix products, arithmetic and copies ran while one was open for 49% of the time, Pallas kernels for 0%

commit v1 on v0

v1 whole, which is shorter than its diff:
```python
import functools

import jax
import jax.numpy as jnp
from jax import lax
from jax.experimental import pallas as pl
from jax.experimental.pallas import tpu as pltpu
from jax.sharding import PartitionSpec as P

HEAD_DIM = 64
TILE = 256
SEGMENTS = 5
MASKED = -1e30
VMEM_LIMIT = 60 * 1024 * 1024
BF16 = jnp.bfloat16
F32 = jnp.float32


def lower(values):
    return values.astype(BF16)


def dot(left, right):
    return lax.dot_general(left, right, (((1,), (0,)), ((), ())), preferred_element_type=F32)


def dot_bt(left, right):
    return lax.dot_general(left, right, (((1,), (1,)), ((), ())), preferred_element_type=F32)


def dot_at(left, right):
    return lax.dot_general(left, right, (((0,), (0,)), ((), ())), preferred_element_type=F32)


def standardise(values):
    centred = values - jnp.mean(values, -1, keepdims=True)
    inverse = lax.rsqrt(jnp.mean(centred * centred, -1, keepdims=True) + 1e-05)
    return centred * inverse, inverse


def norm_back(xhat, inverse, gain, incoming):
    dz = incoming * gain
    inner = jnp.mean(dz * xhat, -1, keepdims=True)
    return (dz - jnp.mean(dz, -1, keepdims=True) - xhat * inner) * inverse


def fold_rows(values):
    rows, width = values.shape
    return jnp.sum(values.reshape(rows // 8, 8, width), axis=0)


def segment_bounds(ids):
    order = jnp.where(ids < 0, SEGMENTS - 1, ids).reshape(1, -1)
    level = lax.broadcasted_iota(jnp.int32, (8, 1), 0)
    return jnp.sum((order < level).astype(jnp.int32), axis=1)


def lane_index(rows):
    return lax.broadcasted_iota(jnp.int32, (rows, 128), 1)


def row_index(rows):
    return lax.broadcasted_iota(jnp.int32, (rows, 128), 0)


def stack_heads(pair, first):
    zero = jnp.zeros_like(pair)
    return jnp.concatenate([jnp.where(first, pair, zero), jnp.where(first, zero, pair)], axis=0)


def each_query_tile(bounds, q_row, k_row, length, visit):
    def per_segment(s, carry):
        q_low, q_high = bounds[q_row, s], bounds[q_row, s + 1]
        k_low, k_high = bounds[k_row, s], bounds[k_row, s + 1]
        q_base, k_base = (q_low // 16) * 16, (k_low // 16) * 16
        q_tiles = (q_high - q_base + TILE - 1) // TILE
        k_tiles = (k_high - k_base + TILE - 1) // TILE

        def per_tile(i, inner):
            low = jnp.maximum(q_low, q_base + i * TILE)
            start = pl.multiple_of(jnp.minimum(q_base + i * TILE, length - TILE), 16)
            visit(start, low, q_high, k_base, k_low, k_high, k_tiles)
            return inner

        return lax.fori_loop(0, q_tiles, per_tile, carry)

    lax.fori_loop(0, SEGMENTS, per_segment, 0)


def key_tile(j, k_base, k_low, k_high, length):
    low = jnp.maximum(k_low, k_base + j * TILE)
    start = pl.multiple_of(jnp.minimum(k_base + j * TILE, length - TILE), 16)
    rows = row_index(TILE) + start
    return start, (rows >= low) & (rows < k_high)


def attend(bounds, q_row, k_row, query, keys, values, out_ref, stat_ref):
    (q_ref, q_col), (k_ref, k_col), (v_ref, v_col) = query, keys, values
    length, width = out_ref.shape
    first = lane_index(TILE) < HEAD_DIM
    lanes = lane_index(TILE)
    unit = jnp.where(lane_index(2 * TILE) == 0, 1.0, 0.0).astype(BF16)
    ones = jnp.ones((TILE, 128), BF16)

    def visit(start, low, high, k_base, k_low, k_high, k_tiles):
        rows = row_index(TILE) + start
        keep = (rows >= low) & (rows < high)
        span = pl.ds(start, TILE)

        def piece(p, k_start, inside):
            cols = p * 128
            bias = jnp.where((lanes == 0) & jnp.logical_not(inside), MASKED, 0.0).astype(BF16)
            queries = stack_heads(q_ref[span, q_col + cols : q_col + cols + 128], first)
            k_span = pl.ds(k_start, TILE)
            pair_k = k_ref[k_span, k_col + cols : k_col + cols + 128]
            pair_v = v_ref[k_span, v_col + cols : v_col + cols + 128]
            scores = dot_bt(
                jnp.concatenate([queries, unit], axis=1), jnp.concatenate([pair_k, bias], axis=1)
            )
            return scores, jnp.concatenate([pair_v, ones], axis=1)

        def finish(p, highest, total):
            cols = p * 128
            mass = total[:, 128:]
            result = total[:, :128] / mass
            log_total = highest + jnp.log(mass)
            merged = lower(jnp.where(first, result[:TILE], result[TILE:]))
            out_ref[span, cols : cols + 128] = jnp.where(
                keep, merged, out_ref[span, cols : cols + 128]
            )
            old = stat_ref[span, :]
            new = jnp.where(lanes == 2 * p, log_total[:TILE], old)
            new = jnp.where(lanes == 2 * p + 1, log_total[TILE:], new)
            stat_ref[span, :] = jnp.where(keep, new, old)

        @pl.when(k_tiles == 1)
        def _():
            k_start, inside = key_tile(0, k_base, k_low, k_high, length)
            for p in range(width // 128):
                scores, wide_v = piece(p, k_start, inside)
                highest = jnp.max(scores, -1, keepdims=True)
                finish(p, highest, dot(lower(jnp.exp(scores - highest)), wide_v))

        @pl.when(k_tiles > 1)
        def _():
            for p in range(width // 128):

                def per_key(j, carry):
                    highest, total = carry
                    k_start, inside = key_tile(j, k_base, k_low, k_high, length)
                    scores, wide_v = piece(p, k_start, inside)
                    newest = jnp.maximum(highest, jnp.max(scores, -1, keepdims=True))
                    expon = lower(jnp.exp(scores - newest))
                    return newest, total * jnp.exp(highest - newest) + dot(expon, wide_v)

                empty = (jnp.full((2 * TILE, 1), MASKED, F32), jnp.zeros((2 * TILE, 256), F32))
                finish(p, *lax.fori_loop(0, k_tiles, per_key, empty))

    each_query_tile(bounds, q_row, k_row, length, visit)


def spread_lanes(column, lanes, lead):
    high = lower(column).astype(F32)
    rest = column - high
    middle = lower(rest).astype(F32)
    spread = jnp.where(lanes == 1, high, jnp.where(lanes == 2, middle, rest - middle))
    return lower(jnp.where(lanes == 0, lead, jnp.where(lanes < 4, -spread, 0.0)))


def attend_back(bounds, q_row, k_row, query, keys, values, do_ref, out_ref, stat_ref, dq, dk, dv):
    (q_ref, q_col), (k_ref, k_col), (v_ref, v_col) = query, keys, values
    (dq_ref, dq_col), (dk_ref, dk_col), (dv_ref, dv_col) = dq, dk, dv
    length, width = do_ref.shape
    first = lane_index(TILE) < HEAD_DIM
    lanes = lane_index(TILE)
    lanes_two = lane_index(2 * TILE)

    def visit(start, low, high, k_base, k_low, k_high, k_tiles):
        rows = row_index(TILE) + start
        keep = (rows >= low) & (rows < high)
        span = pl.ds(start, TILE)

        def per_key(j, carry):
            k_start, inside = key_tile(j, k_base, k_low, k_high, length)
            k_span = pl.ds(k_start, TILE)
            tail = jnp.where(lanes == 0, jnp.where(inside, 0.0, MASKED), 0.0)
            tail = lower(jnp.where((lanes > 0) & (lanes < 4), 1.0, tail))
            for p in range(width // 128):
                cols = p * 128
                pair_q = q_ref[span, q_col + cols : q_col + cols + 128]
                pair_k = k_ref[k_span, k_col + cols : k_col + cols + 128]
                pair_v = v_ref[k_span, v_col + cols : v_col + cols + 128]
                pair_do = jnp.where(keep, do_ref[span, cols : cols + 128], jnp.zeros((), BF16))
                inner = pair_do.astype(F32) * out_ref[span, cols : cols + 128].astype(F32)
                centre = jnp.concatenate(
                    [
                        jnp.sum(jnp.where(first, inner, 0.0), -1, keepdims=True),
                        jnp.sum(jnp.where(first, 0.0, inner), -1, keepdims=True),
                    ],
                    axis=0,
                )
                stat = jnp.where(keep, stat_ref[span, :], -MASKED)
                log_total = jnp.concatenate(
                    [stat[:, 2 * p : 2 * p + 1], stat[:, 2 * p + 1 : 2 * p + 2]], axis=0
                )
                queries = stack_heads(pair_q, first)
                grads = stack_heads(pair_do, first)
                probs = jnp.exp(
                    dot_bt(
                        jnp.concatenate([pair_k, tail], axis=1),
                        jnp.concatenate([queries, spread_lanes(log_total, lanes_two, 1.0)], axis=1),
                    )
                )
                slope = dot_bt(
                    jnp.concatenate([pair_v, tail], axis=1),
                    jnp.concatenate([grads, spread_lanes(centre, lanes_two, 0.0)], axis=1),
                )
                ds = lower(probs * slope)
                dv_ref[k_span, dv_col + cols : dv_col + cols + 128] += dot(lower(probs), grads)
                dk_ref[k_span, dk_col + cols : dk_col + cols + 128] += dot(ds, queries)
                turned = dot(pair_k.T, ds)
                turned = jnp.concatenate(
                    [turned[:HEAD_DIM, :TILE], turned[HEAD_DIM:, TILE:]], axis=0
                )
                dq_ref[span, dq_col + cols : dq_col + cols + 128] += turned.T
            return carry

        lax.fori_loop(0, k_tiles, per_key, 0)

    each_query_tile(bounds, q_row, k_row, length, visit)


def project_kernel(x1, x2, mem, gain, shift, w_qkv, w_kv, xs, qkv, kv):
    width = x1.shape[1]
    both = jnp.concatenate([x1[...], x2[...]], axis=0)
    half = x1.shape[0]
    xs[0] = both[:half]
    xs[1] = both[half:]
    xhat, _ = standardise(both.astype(F32))
    h1 = lower(xhat * gain[0:1, :] + shift[0:1, :])
    for c in range(w_qkv.shape[1] // width):
        cols = slice(c * width, (c + 1) * width)
        part = dot(h1, w_qkv[:, cols])
        if c == 0:
            part = part * HEAD_DIM ** (-0.5)
        part = lower(part)
        qkv[0, :, cols] = part[:half]
        qkv[1, :, cols] = part[half:]
    kv[...] = lower(dot(mem[...], w_kv[...]))


def forward_kernel(
    bounds, xs, qkv, kv, gain, shift, w_self, w_query, a1, y1, q2, a2, stat1, stat2
):
    length, width = a1.shape[1:]
    attend(
        bounds,
        0,
        0,
        (qkv.at[0], 0),
        (qkv.at[0], width),
        (qkv.at[0], 2 * width),
        a1.at[0],
        stat1.at[0],
    )

    def rows(i, carry):
        span = pl.ds(pl.multiple_of(i * TILE, TILE), TILE)
        after = xs[0, span, :].astype(F32) + dot(a1[0, span, :], w_self[...])
        y1[0, span, :] = after
        xhat, _ = standardise(after)
        h2 = lower(xhat * gain[1:2, :] + shift[1:2, :])
        q2[0, span, :] = lower(dot(h2, w_query[...]) * HEAD_DIM ** (-0.5))
        return carry

    lax.fori_loop(0, length // TILE, rows, 0)
    attend(bounds, 0, 1, (q2.at[0], 0), (kv, 0), (kv, width), a2.at[0], stat2.at[0])


def feed_kernel(
    per_step, y1, a2, g1, g2, gain, shift, w_cross, w_in, w_out,
    o1, o2, h3, r, du, e2, dy2, do2, dnorm,
):
    i = pl.program_id(0)
    width = w_cross.shape[0]
    is_first = i < per_step
    grad = jnp.where(is_first, g1[...], g2[...])
    after = y1[0] + dot(a2[0], w_cross[...])
    xhat, inverse = standardise(after)
    normed = lower(xhat * gain[2:3, :] + shift[2:3, :])
    h3[0] = normed
    result = after
    dh3 = jnp.zeros_like(after)
    slope = (2.0 / jnp.pi) ** 0.5
    for c in range(w_in.shape[1] // width):
        cols = slice(c * width, (c + 1) * width)
        u = dot(normed, w_in[:, cols])
        dr = dot_bt(grad, w_out[cols, :])
        square = u * u
        t = jnp.tanh(slope * (u + 0.044715 * (square * u)))
        half = 0.5 * (1.0 + t)
        hidden = lower(u * half)
        r[0, :, cols] = hidden
        gate = half + 0.5 * u * (1.0 - t * t) * (slope * (1.0 + 3 * 0.044715 * square))
        pre = lower(dr * gate)
        du[0, :, cols] = pre
        result = result + dot(hidden, w_out[cols, :])
        dh3 = dh3 + dot_bt(pre, w_in[:, cols])

    @pl.when(is_first)
    def _():
        o1[...] = lower(result)

    @pl.when(jnp.logical_not(is_first))
    def _():
        o2[...] = lower(result)

    @pl.when(i == 0)
    def _():
        dnorm[...] = jnp.zeros_like(dnorm)

    dnorm[0] += fold_rows(dh3 * xhat)
    dnorm[1] += fold_rows(dh3)
    back = grad.astype(F32) + norm_back(xhat, inverse, gain[2:3, :], dh3)
    dy2[0] = back
    low = lower(back)
    e2[0] = low
    do2[0] = lower(dot_bt(low, w_cross[...]))


def feed_grad_kernel(h3, a2, e2, g1, g2, du, r, d_in, d_out, d_cross, turned):
    c = pl.program_id(0)
    half = g1.shape[0]

    @pl.when(c == 0)
    def _():
        turned[...] = h3[...].T
        d_cross[...] = lower(dot(a2[...].T, e2[...]))

    d_in[...] = lower(dot(turned[...], du[...]))
    d_out[...] = lower(dot_at(r[:half, :], g1[...]) + dot_at(r[half:, :], g2[...]))


def cross_back_kernel(
    bounds, q2, kv, a1, a2, stat2, do2, y1, dy2, mem, gain, shift, w_query, w_self, w_kv,
    dy1, do1, d_query, d_self, d_kv, d_mem, dnorm,
    dq_sum, dkv_sum, h2, low_q, low_e,
):
    step = pl.program_id(0)
    length, width = q2.shape[1:]

    @pl.when(step == 0)
    def _():
        dkv_sum[...] = jnp.zeros_like(dkv_sum)
        dnorm[...] = jnp.zeros_like(dnorm)

    dq_sum[...] = jnp.zeros_like(dq_sum)
    attend_back(
        bounds, 0, 1, (q2.at[0], 0), (kv, 0), (kv, width), do2.at[0], a2.at[0], stat2.at[0],
        (dq_sum, 0), (dkv_sum, 0), (dkv_sum, width),
    )

    def rows(i, carry):
        span = pl.ds(pl.multiple_of(i * TILE, TILE), TILE)
        grad_q = lower(dq_sum[span, :] * HEAD_DIM ** (-0.5))
        low_q[step, span, :] = grad_q
        xhat, inverse = standardise(y1[0, span, :])
        h2[step, span, :] = lower(xhat * gain[1:2, :] + shift[1:2, :])
        dh2 = dot_bt(grad_q, w_query[...])
        dnorm[0] += fold_rows(dh2 * xhat)
        dnorm[1] += fold_rows(dh2)
        back = dy2[0, span, :] + norm_back(xhat, inverse, gain[1:2, :], dh2)
        dy1[0, span, :] = back
        low = lower(back)
        low_e[step, span, :] = low
        do1[0, span, :] = lower(dot_bt(low, w_self[...]))
        return carry

    lax.fori_loop(0, length // TILE, rows, 0)

    @pl.when(step == 1)
    def _():
        d_query[...] = lower(dot(h2[0].T, low_q[0]) + dot(h2[1].T, low_q[1]))
        d_self[...] = lower(dot(a1[0].T, low_e[0]) + dot(a1[1].T, low_e[1]))
        pair = lower(dkv_sum[...])
        d_kv[...] = lower(dot(mem[...].T, pair))
        d_mem[...] = dot_bt(pair, w_kv[...])


def self_back_kernel(
    bounds, xs, qkv, a1, stat1, do1, dy1, gain, shift, w_qkv,
    gi1, gi2, d_qkv, dnorm,
    sums, h1, low,
):
    step = pl.program_id(0)
    length, width = do1.shape[1:]

    @pl.when(step == 0)
    def _():
        dnorm[...] = jnp.zeros_like(dnorm)

    sums[...] = jnp.zeros_like(sums)
    attend_back(
        bounds, 0, 0, (qkv.at[0], 0), (qkv.at[0], width), (qkv.at[0], 2 * width),
        do1.at[0], a1.at[0], stat1.at[0], (sums, 0), (sums, width), (sums, 2 * width),
    )

    def rows(i, carry):
        span = pl.ds(pl.multiple_of(i * TILE, TILE), TILE)
        low[step, span, :width] = lower(sums[span, :width] * HEAD_DIM ** (-0.5))
        low[step, span, width:] = lower(sums[span, width:])
        xhat, inverse = standardise(xs[0, span, :].astype(F32))
        h1[step, span, :] = lower(xhat * gain[0:1, :] + shift[0:1, :])
        dh1 = dot_bt(low[step, span, :], w_qkv[...])
        dnorm[0] += fold_rows(dh1 * xhat)
        dnorm[1] += fold_rows(dh1)
        back = dy1[0, span, :] + norm_back(xhat, inverse, gain[0:1, :], dh1)

        @pl.when(step == 0)
        def _():
            gi1[span, :] = back

        @pl.when(step == 1)
        def _():
            gi2[span, :] = back

        return carry

    lax.fori_loop(0, length // TILE, rows, 0)

    @pl.when(step == 1)
    def _():
        d_qkv[...] = lower(dot(h1[0].T, low[0]) + dot(h1[1].T, low[1]))


def whole(shape):
    zeros = (0,) * len(shape)
    return pl.BlockSpec(shape, lambda *_: zeros, pipeline_mode=pl.Buffered(1))


def fixed(shape):
    zeros = (0,) * len(shape)
    return pl.BlockSpec(shape, lambda *_: zeros)


def by_step(shape):
    return pl.BlockSpec((1,) + shape, lambda t, *_: (t, 0, 0))


def params():
    return pltpu.CompilerParams(
        vmem_limit_bytes=VMEM_LIMIT, dimension_semantics=("arbitrary",)
    )


def struct(shape, dtype):
    return jax.ShapeDtypeStruct(shape, dtype)


def local_step(x1, x2, mem, g1, g2, target_ids, memory_ids, gain, shift, weights):
    w_qkv, w_self, w_query, w_kv, w_cross, w_in, w_out = weights
    length, width = x1.shape
    hidden = w_in.shape[1]
    tiles = length // TILE
    bounds = jnp.stack([segment_bounds(target_ids), segment_bounds(memory_ids)])
    norm_spec = whole((3, width))
    row_tile = pl.BlockSpec((TILE, width), lambda i: (i, 0))

    xs, qkv, kv = pl.pallas_call(
        project_kernel,
        grid=(tiles,),
        in_specs=[row_tile, row_tile, row_tile, norm_spec, norm_spec, whole(w_qkv.shape), whole(w_kv.shape)],
        out_specs=[
            pl.BlockSpec((2, TILE, width), lambda i: (0, i, 0)),
            pl.BlockSpec((2, TILE, 3 * width), lambda i: (0, i, 0)),
            pl.BlockSpec((TILE, 2 * width), lambda i: (i, 0)),
        ],
        out_shape=[
            struct((2, length, width), BF16),
            struct((2, length, 3 * width), BF16),
            struct((length, 2 * width), BF16),
        ],
        compiler_params=params(),
        name="project",
    )(x1, x2, mem, gain, shift, w_qkv, w_kv)

    step_low = by_step((length, width))
    a1, y1, q2, a2, stat1, stat2 = pl.pallas_call(
        forward_kernel,
        grid_spec=pltpu.PrefetchScalarGridSpec(
            num_scalar_prefetch=1,
            grid=(2,),
            in_specs=[
                step_low, by_step((length, 3 * width)), whole(kv.shape), norm_spec, norm_spec,
                whole(w_self.shape), whole(w_query.shape),
            ],
            out_specs=[step_low] * 4 + [by_step((length, 128))] * 2,
        ),
        out_shape=[
            struct((2, length, width), BF16),
            struct((2, length, width), F32),
            struct((2, length, width), BF16),
            struct((2, length, width), BF16),
            struct((2, length, 128), F32),
            struct((2, length, 128), F32),
        ],
        compiler_params=params(),
        name="attend_forward",
    )(bounds, xs, qkv, kv, gain, shift, w_self, w_query)

    step_tile = pl.BlockSpec((1, TILE, width), lambda i: (i // tiles, i % tiles, 0))
    step_wide = pl.BlockSpec((1, TILE, hidden), lambda i: (i // tiles, i % tiles, 0))
    early = pl.BlockSpec((TILE, width), lambda i: (jnp.minimum(i, tiles - 1), 0))
    late = pl.BlockSpec((TILE, width), lambda i: (jnp.maximum(i - tiles, 0), 0))
    o1, o2, h3, r, du, e2, dy2, do2, dnorm2 = pl.pallas_call(
        functools.partial(feed_kernel, tiles),
        grid=(2 * tiles,),
        in_specs=[
            step_tile, step_tile, early, late, norm_spec, norm_spec,
            whole(w_cross.shape), whole(w_in.shape), whole(w_out.shape),
        ],
        out_specs=[
            early, late, step_tile, step_wide, step_wide, step_tile, step_tile, step_tile,
            fixed((2, 8, width)),
        ],
        out_shape=[
            struct((length, width), BF16),
            struct((length, width), BF16),
            struct((2, length, width), BF16),
            struct((2, length, hidden), BF16),
            struct((2, length, hidden), BF16),
            struct((2, length, width), BF16),
            struct((2, length, width), F32),
            struct((2, length, width), BF16),
            struct((2, 8, width), F32),
        ],
        compiler_params=params(),
        name="feed_forward_back",
    )(y1, a2, g1, g2, gain, shift, w_cross, w_in, w_out)

    flat = (2 * length, width)
    chunk = pl.BlockSpec((2 * length, width), lambda c: (0, c))
    d_in, d_out, d_cross = pl.pallas_call(
        feed_grad_kernel,
        grid=(hidden // width,),
        in_specs=[whole(flat), whole(flat), whole(flat), whole((length, width)), whole((length, width)), chunk, chunk],
        out_specs=[
            pl.BlockSpec((width, width), lambda c: (0, c)),
            pl.BlockSpec((width, width), lambda c: (c, 0)),
            fixed((width, width)),
        ],
        out_shape=[
            struct((width, hidden), BF16),
            struct((hidden, width), BF16),
            struct((width, width), BF16),
        ],
        scratch_shapes=[pltpu.VMEM((width, 2 * length), BF16)],
        compiler_params=params(),
        name="feed_weight_grads",
    )(h3.reshape(flat), a2.reshape(flat), e2.reshape(flat), g1, g2, du.reshape(2 * length, hidden), r.reshape(2 * length, hidden))

    dy1, do1, d_query, d_self, d_kv, d_mem, dnorm1 = pl.pallas_call(
        cross_back_kernel,
        grid_spec=pltpu.PrefetchScalarGridSpec(
            num_scalar_prefetch=1,
            grid=(2,),
            in_specs=[
                step_low, whole(kv.shape), whole(a1.shape), step_low, by_step((length, 128)), step_low,
                step_low, step_low, whole(mem.shape), norm_spec, norm_spec,
                whole(w_query.shape), whole(w_self.shape), whole(w_kv.shape),
            ],
            out_specs=[
                step_low, step_low, fixed((width, width)), fixed((width, width)), fixed((width, 2 * width)),
                fixed((length, width)), fixed((2, 8, width)),
            ],
            scratch_shapes=[
                pltpu.VMEM((length, width), F32),
                pltpu.VMEM((length, 2 * width), F32),
                pltpu.VMEM((2, length, width), BF16),
                pltpu.VMEM((2, length, width), BF16),
                pltpu.VMEM((2, length, width), BF16),
            ],
        ),
        out_shape=[
            struct((2, length, width), F32),
            struct((2, length, width), BF16),
            struct((width, width), BF16),
            struct((width, width), BF16),
            struct((width, 2 * width), BF16),
            struct((length, width), F32),
            struct((2, 8, width), F32),
        ],
        compiler_params=params(),
        name="cross_back",
    )(bounds, q2, kv, a1, a2, stat2, do2, y1, dy2, mem, gain, shift, w_query, w_self, w_kv)

    gi1, gi2, d_qkv, dnorm0 = pl.pallas_call(
        self_back_kernel,
        grid_spec=pltpu.PrefetchScalarGridSpec(
            num_scalar_prefetch=1,
            grid=(2,),
            in_specs=[
                step_low, by_step((length, 3 * width)), step_low, by_step((length, 128)), step_low, step_low,
                norm_spec, norm_spec, whole(w_qkv.shape),
            ],
            out_specs=[
                fixed((length, width)), fixed((length, width)), fixed((width, 3 * width)), fixed((2, 8, width)),
            ],
            scratch_shapes=[
                pltpu.VMEM((length, 3 * width), F32),
                pltpu.VMEM((2, length, width), BF16),
                pltpu.VMEM((2, length, 3 * width), BF16),
            ],
        ),
        out_shape=[
            struct((length, width), F32),
            struct((length, width), F32),
            struct((width, 3 * width), BF16),
            struct((2, 8, width), F32),
        ],
        compiler_params=params(),
        name="self_back",
    )(bounds, xs, qkv, a1, stat1, do1, dy1, gain, shift, w_qkv)

    dnorm = jnp.sum(jnp.stack([dnorm0, dnorm1, dnorm2]), axis=2)
    return o1, o2, gi1, gi2, d_mem, dnorm, (d_qkv, d_self, d_query, d_kv, d_cross, d_in, d_out)


def body(
    inputs_one, inputs_two, memory, cotangent_one, cotangent_two, target_ids, memory_ids,
    norm_gain, norm_shift, self_qkv, self_out, cross_query, cross_kv, cross_out, ffn_in, ffn_out,
):
    shape = inputs_one.shape
    length, width = shape[1:]
    norms = lax.all_gather(jnp.concatenate([norm_gain, norm_shift]), "wide", axis=1, tiled=True).astype(F32)
    weights = tuple(
        lax.all_gather(item, "wide", axis=0, tiled=True)
        for item in (self_qkv, self_out, cross_query, cross_kv, cross_out, ffn_in, ffn_out)
    )
    o1, o2, gi1, gi2, d_mem, dnorm, grads = local_step(
        inputs_one.reshape(length, width),
        inputs_two.reshape(length, width),
        memory.reshape(length, width),
        cotangent_one.reshape(length, width),
        cotangent_two.reshape(length, width),
        target_ids,
        memory_ids,
        norms[:3],
        norms[3:],
        weights,
    )
    shares = [lax.psum_scatter(item, "wide", scatter_dimension=0, tiled=True) for item in grads]
    norm_rows = jnp.concatenate([dnorm[:, 0], dnorm[:, 1]])
    norm_share = lax.psum_scatter(norm_rows.astype(BF16), "wide", scatter_dimension=1, tiled=True)
    totals = [lax.psum(item, "narrow").astype(F32) for item in shares + [norm_share]]
    return (
        o1.reshape(shape), o2.reshape(shape), gi1.reshape(shape), gi2.reshape(shape), d_mem.reshape(shape),
        totals[7][:3], totals[7][3:],
        totals[0], totals[1], totals[2], totals[3], totals[4], totals[5], totals[6],
    )


def solution(mesh):
    rows = P(("narrow", "wide"), None, None)
    ids = P(("narrow", "wide"), None)
    norm, weight = P(None, "wide"), P("wide", None)
    return jax.shard_map(
        body,
        mesh=mesh,
        in_specs=(rows,) * 5 + (ids,) * 2 + (norm,) * 2 + (weight,) * 7,
        out_specs=(rows,) * 5 + (norm,) * 2 + (weight,) * 7,
        check_vma=False,
    )
```

time: 1080 us -> 566 us (0.52)
  matrix products: 449 us -> 0 us
  Pallas kernels: 0 us -> 223 us
  local copies, waits for them, and re-layouts: 180 us -> 2.93 us
  other arithmetic: 182 us -> 11 us
  waiting for transfers between devices: 154 us -> 240 us
    dot_general x95 -> x0, matrix products: 449 us -> none  [the longest x16 125 us: masked_scores(): jnp.einsum('sqhe,skhe->shqk', query_block, keys, preferred_element_type=j...]
    pallas_call x0 -> x6, Pallas kernels: none -> 223 us  [the longest x1 61.7 us: local_step(): pl.pallas_call(cross_back_kernel, grid_spec=pltpu.PrefetchScalarGridSpec(...]
    reduce_scatter x6 -> x7, waiting for transfers between devices: 64 us -> 158 us  [body(): lax.psum_scatter(item, 'wide', scatter_dimension=0, tiled=True)]
    convert_element_type x24 -> x8, other arithmetic: 89.6 us -> 8.05 us  [the longest x7 8.04 us: body(): lax.psum(item, 'narrow').astype(F32)]
    reduce_sum x24 -> x3, other arithmetic: 57.4 us -> 0.29 us  [the longest x2 0.25 us: segment_bounds(): return jnp.sum((order < level).astype(jnp.int32), axis=1)]
    unnamed x355 -> x19, local copies, waits for them, and re-layouts: 56.8 us -> 1.65 us
    another operation x22 -> x0, local copies, waits for them, and re-layouts: 38.9 us -> none  [the longest x8 25.5 us: blocks_of(): return jnp.moveaxis(moved, 1, 0)]
    while x172 -> x0, local copies, waits for them, and re-layouts: 31.2 us -> none
  transfers between devices with their start and end apart: 14 -> 13, of which waited for: 5 -> 7; matrix products, arithmetic and copies ran while one was open for 49% -> 1% of each run, Pallas kernels for 0% -> 30%
where the time goes in v1:
time: 566 us
  waiting for transfers between devices  240 us (42%)
  Pallas kernels  223 us (39%)
  blocking collectives  74.6 us (13%)
  between operations  14.1 us (2%)
  other arithmetic  11 us (2%)
    reduce_scatter x7, waiting for transfers between devices, body(): lax.psum_scatter(item, 'wide', scatter_dimension=0, tiled=True)  158 us
    pallas_call x1, Pallas kernels, local_step(): pl.pallas_call(cross_back_kernel, grid_spec=pltpu.PrefetchScalarGridSpec(...  61.7 us
    pallas_call x1, Pallas kernels, local_step(): pl.pallas_call(self_back_kernel, grid_spec=pltpu.PrefetchScalarGridSpec(n...  60.2 us
    all_gather x3, blocking collectives, body(): lax.all_gather(item, 'wide', axis=0, tiled=True)  50.3 us
    psum x1, waiting for transfers between devices, body(): lax.psum(item, 'narrow').astype(F32)  44.5 us
    pallas_call x1, Pallas kernels, local_step(): pl.pallas_call(forward_kernel, grid_spec=pltpu.PrefetchScalarGridSpec(num...  38.2 us
    pallas_call x1, Pallas kernels, local_step(): pl.pallas_call(functools.partial(feed_kernel, tiles), grid=(2 * tiles,),...  37 us
    unnamed x14, waiting for transfers between devices  36.8 us
  transfers between devices with their start and end apart: 13, of which 7 were waited for; matrix products, arithmetic and copies ran while one was open for 1% of the time, Pallas kernels for 30%

profile of v1, /device:TPU:0, one launch (start us, length us, event | category | flops | bytes accessed | tf_op | source)
XLA Modules:
  0.0 566.1 jit_solution(15474851862289481532)
XLA Ops:
  7.2 0.7 all-gather.8.cloned.1.call-update
  8.0 0.7 all-gather.6.cloned.1.call-update
  8.7 0.7 all-gather.10.cloned.1.call-update
  9.5 0.5 all-gather.12.cloned.1.call-update
  10.0 0.7 maximum_bitcast_fusion
  10.7 14.5 %all-gather = bf16[8,64,6]{1,2,0:T(8,128)(2,1)S(1)} all-gather(bf16[1,64,6]{1,2,0:T(8,128)(2,1)S(1)} %maximum_bitcast_fusion), channel_id=1, replica_groups=mesh['narrow'=4,'wide'=8] {'wide'}, dimensions={0}, use_global_device_ids=true | all-gather | bytes 6912 | tf_op jit(solution)/shard_map/all_gather | solution.py:635
  25.2 0.1 reshape.90
  25.3 0.7 compare_select_fusion.1
  26.0 0.1 convert_reduce_fusion.1
  26.1 0.7 compare_select_fusion
  26.8 0.1 convert_reduce_fusion
  26.9 0.6 pad_add_fusion.bounds
  27.5 0.6 fusion
  28.1 16.5 %all_gather.27.w_self = bf16[512,512]{1,0:T(8,128)(2,1)} all-gather(bf16[64,512]{1,0:T(8,128)(2,1)} %param.26), channel_id=1, replica_groups=mesh['narrow'=4,'wide'=8] {'wide'}, dimensions={0}, use_global_device_ids=true | all-gather | bytes 589824 | tf_op jit(solution)/shard_map/all_gather | solution.py:637
  44.6 18.0 %all_gather.28.w_query = bf16[512,512]{1,0:T(8,128)(2,1)} all-gather(bf16[64,512]{1,0:T(8,128)(2,1)} %param.27), channel_id=1, replica_groups=mesh['narrow'=4,'wide'=8] {'wide'}, dimensions={0}, use_global_device_ids=true | all-gather | bytes 589824 | tf_op jit(solution)/shard_map/all_gather | solution.py:637
  62.6 15.8 %all_gather.29.w_cross = bf16[512,512]{1,0:T(8,128)(2,1)} all-gather(bf16[64,512]{1,0:T(8,128)(2,1)S(1)} %copy-done.1), channel_id=1, replica_groups=mesh['narrow'=4,'wide'=8] {'wide'}, dimensions={0}, use_global_device_ids=true | all-gather | bytes 589824 | tf_op jit(solution)/shard_map/all_gather | solution.py:637
  78.4 9.9 %project.1 = (bf16[2,1024,512]{2,1,0:T(8,128)(2,1)}, bf16[2,1024,1536]{2,1,0:T(8,128)(2,1)}, bf16[1024,1024]{1,0:T(8,128)(2,1)}) custom-call(bf16[1024,512]{1,0:T(8,128)(2,1)} %bitcast.46, bf16[1024,512]{1,0:T(8,128)(2,1)} %bitcast.47, bf16[1024,512]{1,0:T(8,128)(2,1)} %bitcast.42, f32[3,512]{1,0:T(4,128)} %get-tuple-element.86.gain, ...), custom_call_target="tpu_custom_call" | custom-call | tf_op jit(solution)/shard_map/project/pallas_call | solution.py:469
  88.3 38.2 %attend_forward.1 = (bf16[2,1024,512]{2,1,0:T(8,128)(2,1)}, f32[2,1024,512]{2,1,0:T(8,128)}, bf16[2,1024,512]{2,1,0:T(8,128)(2,1)}, bf16[2,1024,512]{2,1,0:T(8,1...) custom-call(s32[2,8]{1,0:T(2,128)} %pad_add_fusion.bounds, bf16[2,1024,512]{2,1,0:T(8,128)(2,1)} %get-tuple-element.46.xs, ...), custom_call_target="tpu_custom_call" | custom-call | tf_op jit(solution)/shard_map/attend_forward/pallas_call | solution.py:488
  126.5 37.0 %feed_forward_back.1 = (bf16[1024,512]{1,0:T(8,128)(2,1)}, bf16[1024,512]{1,0:T(8,128)(2,1)}, bf16[2,1024,512]{2,1,0:T(8,128)(2,1)}, bf16[2,1024,2048]{2,1,0:T(8...) custom-call(f32[2,1024,512]{2,1,0:T(8,128)} %get-tuple-element.49.y1, ...), custom_call_target="tpu_custom_call" | custom-call | tf_op jit(solution)/shard_map/feed_forward_back/pallas_call | solution.py:515
  163.5 16.4 %feed_weight_grads.1 = (bf16[512,2048]{1,0:T(8,128)(2,1)}, bf16[2048,512]{1,0:T(8,128)(2,1)}, bf16[512,512]{1,0:T(8,128)(2,1)}) custom-call(bf16[2048,512]{1,0:T(8,128)(2,1)} %bitcast.44, bf16[2048,512]{1,0:T(8,128)(2,1)} %bitcast.35, bf16[2048,512]{1,0:T(8,128)(2,1)} %bitcast.45, bf16[1024,512]{1,0:T(8,128)(2,1)} %bitcast.39, bf16[1024,512]{1,0:T(8,128)(2,1)} %bitcast.41, ...), custom_call_target="tpu_custom_call" | custom-call | tf_op jit(solution)/shard_map/feed_weight_grads/pallas_call | solution.py:543
  180.0 0.0 reduce-scatter.13.cloned.1.call-start
  180.0 61.7 %cross_back.1 = (f32[2,1024,512]{2,1,0:T(8,128)}, bf16[2,1024,512]{2,1,0:T(8,128)(2,1)}, bf16[512,512]{1,0:T(8,128)(2,1)}, bf16[512,512]{1,0:T(8,128)(2,1)}, bf1...) custom-call(s32[2,8]{1,0:T(2,128)} %pad_add_fusion.bounds, ...), custom_call_target="tpu_custom_call" | custom-call | tf_op jit(solution)/shard_map/cross_back/pallas_call | solution.py:562
  241.8 0.0 reduce-scatter.15.cloned.1.call-start
  241.8 0.7 reduce-scatter.15.cloned.1.call-update
  242.6 0.7 reduce-scatter.17.cloned.1.call-update
  243.3 60.2 %self_back.1 = (f32[1024,512]{1,0:T(8,128)}, f32[1024,512]{1,0:T(8,128)}, bf16[512,1536]{1,0:T(8,128)(2,1)}, f32[2,8,512]{2,1,0:T(8,128)}) custom-call(s32[2,8]{1,0:T(2,128)} %pad_add_fusion.bounds, bf16[2,1024,512]{2,1,0:T(8,128)(2,1)} %get-tuple-element.46.xs, bf16[2,1024,1536]{2,1,0:T(8,128)(2,1)} %get-tuple-element.47.qkv, ...), custom_call_target="tpu_custom_call" | custom-call | tf_op jit(solution)/shard_map/self_back/pallas_call | solution.py:597
  303.5 0.0 reduce-scatter.21.cloned.1.call-start
  303.6 0.5 reduce-scatter.21.cloned.1.call-update
  304.1 0.7 reduce-scatter.23.cloned.1.call-update
  305.0 0.8 copy.37
  305.8 0.0 all-reduce.3.cloned.1.call-start
  305.9 17.3 %reduce-scatter.15.cloned.1.call-done = bf16[64,512]{1,0:T(8,128)(2,1)} async-done(((bf16[512,512]{1,0:T(8,128)(2,1)}), bf16[64,512]{1,0:T(8,128)(2,1)}) %reduce-scatter.15.cloned.1.call-update) | async-done | bytes 65552 | tf_op jit(solution)/shard_map/reduce_scatter | solution.py:652
  323.3 32.7 %reduce-scatter.17.cloned.1.call-done = bf16[64,1024]{1,0:T(8,128)(2,1)} async-done(((bf16[512,1024]{1,0:T(8,128)(2,1)}), bf16[64,1024]{1,0:T(8,128)(2,1)}) %reduce-scatter.17.cloned.1.call-update) | async-done | bytes 131088 | tf_op jit(solution)/shard_map/reduce_scatter | solution.py:652
  356.0 35.0 %reduce-scatter.11.cloned.1.call-done = bf16[64,1536]{1,0:T(8,128)(2,1)} async-done(((bf16[512,1536]{1,0:T(8,128)(2,1)}), bf16[64,1536]{1,0:T(8,128)(2,1)}) %reduce-scatter.11.cloned.1.call-update) | async-done | bytes 196624 | tf_op jit(solution)/shard_map/reduce_scatter | solution.py:652
  391.0 36.0 %reduce-scatter.21.cloned.1.call-done = bf16[64,2048]{1,0:T(8,128)(2,1)} async-done(((bf16[512,2048]{1,0:T(8,128)(2,1)}), bf16[64,2048]{1,0:T(8,128)(2,1)}) %reduce-scatter.21.cloned.1.call-update) | async-done | bytes 262160 | tf_op jit(solution)/shard_map/reduce_scatter | solution.py:652
  427.0 37.1 %reduce-scatter.23.cloned.1.call-done = bf16[256,512]{1,0:T(8,128)(2,1)} async-done(((bf16[2048,512]{1,0:T(8,128)(2,1)}), bf16[256,512]{1,0:T(8,128)(2,1)}) %reduce-scatter.23.cloned.1.call-update) | async-done | bytes 262160 | tf_op jit(solution)/shard_map/reduce_scatter | solution.py:652
  464.1 31.6 %reduce-scatter.25.cloned.1.call-done = bf16[64,6]{1,0:T(8,128)(2,1)} async-done(((bf16[512,6]{1,0:T(8,128)(2,1)}), bf16[64,6]{1,0:T(8,128)(2,1)}) %reduce-scatter.25.cloned.1.call-update) | async-done | bytes 784
  495.7 0.8 copy.38
  496.5 9.9 %psum.56 = bf16[6,64]{1,0:T(8,128)(2,1)S(1)} all-reduce(bf16[6,64]{1,0:T(8,128)(2,1)S(1)} %copy.38), channel_id=1, replica_groups=mesh['narrow'=4,'wide'=8] {'narrow'}, use_global_device_ids=true, to_apply=%region_4.5 | all-reduce | flops 384 | bytes 1536 | tf_op jit(solution)/shard_map/psum | solution.py:655
  506.4 0.6 fusion.2
  507.0 44.5 %all-reduce.3.cloned.1.call-done = (bf16[64,1536]{1,0:T(8,128)(2,1)}, bf16[64,512]{1,0:T(8,128)(2,1)}, bf16[64,512]{1,0:T(8,128)(2,1)}, bf16[64,1024]{1,0:T(8,12...) async-done(((bf16[64,1536]{1,0:T(8,128)(2,1)}, bf16[64,512]{1,0:T(8,128)(2,1)}, bf16[64,512]{1,0:T(8,128)(2,1)}, ...) | async-done | bytes 1048592 | tf_op jit(solution)/shard_map/psum | solution.py:655
  551.5 1.8 convert_element_type.43
  553.3 1.8 convert_element_type.44
  555.1 1.7 convert_element_type.38
  556.8 0.7 convert_element_type.41
  557.5 0.7 convert_element_type.39
  558.2 0.7 convert_element_type.40
  558.9 0.7 convert_element_type.42
  (41 shorter events, 0.6 us)
Async XLA Ops:
  7.2 55.4 %copy-start.1 = (bf16[64,512]{1,0:T(8,128)(2,1)S(1)}, bf16[64,512]{1,0:T(8,128)(2,1)}, u32[]{:S(2)}) copy-start(bf16[64,512]{1,0:T(8,128)(2,1)} %param.29) | copy-start | bytes 196612
  7.2 71.2 %all-gather.8.cloned.1.call-start = ((), (), s32[]{:S(2)}) async-start(), calls=%async_computation.9 | async-start | bytes 1179648 | tf_op jit(solution)/shard_map/all_gather | solution.py:637
  7.9 70.5 %all-gather.6.cloned.1.call-start = ((), (), s32[]{:S(2)}) async-start(), calls=%async_computation.8 | async-start | bytes 1769472 | tf_op jit(solution)/shard_map/all_gather | solution.py:637
  8.7 117.8 %all-gather.10.cloned.1.call-start = ((), (), s32[]{:S(2)}) async-start(), calls=%async_computation.10 | async-start | bytes 2359296 | tf_op jit(solution)/shard_map/all_gather | solution.py:637
  9.4 117.1 %all-gather.12.cloned.1.call-start = ((), (), s32[]{:S(2)}) async-start(), calls=%async_computation.11 | async-start | bytes 2359296 | tf_op jit(solution)/shard_map/all_gather | solution.py:637
  10.0 295.9 %reduce-scatter.19.cloned.1.call-start = ((), (), s32[]{:S(2)}) async-start(), calls=%async_computation.16 | async-start | bytes 589824 | tf_op jit(solution)/shard_map/reduce_scatter | solution.py:652
  180.0 126.0 %reduce-scatter.13.cloned.1.call-start = ((), (), s32[]{:S(2)}) async-start(), calls=%async_computation.13 | async-start | bytes 589824 | tf_op jit(solution)/shard_map/reduce_scatter | solution.py:652
  241.8 81.5 %reduce-scatter.15.cloned.1.call-start = ((), (), s32[]{:S(2)}) async-start(), calls=%async_computation.14 | async-start | bytes 589824 | tf_op jit(solution)/shard_map/reduce_scatter | solution.py:652
  242.5 113.5 %reduce-scatter.17.cloned.1.call-start = ((), (), s32[]{:S(2)}) async-start(), calls=%async_computation.15 | async-start | bytes 1179648 | tf_op jit(solution)/shard_map/reduce_scatter | solution.py:652
  243.3 147.7 %reduce-scatter.11.cloned.1.call-start = ((), (), s32[]{:S(2)}) async-start(), calls=%async_computation.12 | async-start | bytes 1769472 | tf_op jit(solution)/shard_map/reduce_scatter | solution.py:652
  303.5 123.5 %reduce-scatter.21.cloned.1.call-start = ((), (), s32[]{:S(2)}) async-start(), calls=%async_computation.17 | async-start | bytes 2359296 | tf_op jit(solution)/shard_map/reduce_scatter | solution.py:652
  303.6 1.3 copy-start.5
  303.6 1.3 copy-start.6
  303.6 1.3 copy-start.7
  304.1 160.0 %reduce-scatter.23.cloned.1.call-start = ((), (), s32[]{:S(2)}) async-start(), calls=%async_computation.18 | async-start | bytes 2359296 | tf_op jit(solution)/shard_map/reduce_scatter | solution.py:652
  304.8 190.9 %reduce-scatter.25.cloned.1.call-start = ((), (), s32[]{:S(2)}) async-start(), calls=%async_computation.19 | async-start | bytes 147456
  305.8 245.6 %all-reduce.3.cloned.1.call-start = ((), (), s32[]{:S(2)}) async-start(), calls=%async_computation.20 | async-start | bytes 2097152 | tf_op jit(solution)/shard_map/psum | solution.py:655
  551.5 5.3 copy-start
  551.5 6.1 %copy-start.4 = (bf16[64,512]{1,0:T(8,128)(2,1)S(1)}, bf16[64,512]{1,0:T(8,128)(2,1)}, u32[]{:S(2)}) copy-start(bf16[64,512]{1,0:T(8,128)(2,1)} %get-tuple-element.79) | copy-start | bytes 196612
  551.5 6.7 %copy-start.3 = (bf16[64,512]{1,0:T(8,128)(2,1)S(1)}, bf16[64,512]{1,0:T(8,128)(2,1)}, u32[]{:S(2)}) copy-start(bf16[64,512]{1,0:T(8,128)(2,1)} %get-tuple-element.80) | copy-start | bytes 196612
  551.5 7.4 %copy-start.2 = (bf16[64,512]{1,0:T(8,128)(2,1)S(1)}, bf16[64,512]{1,0:T(8,128)(2,1)}, u32[]{:S(2)}) copy-start(bf16[64,512]{1,0:T(8,128)(2,1)} %get-tuple-element.82) | copy-start | bytes 196612
Sparse Core Ops, SparseCore 0:
  9.6 24.9 all-gather.7
  36.3 29.0 all-gather.5
  67.0 28.5 all-gather.9
  97.0 28.9 all-gather.11
  180.1 41.4 reduce-scatter.18
  241.9 49.3 reduce-scatter.12
  294.2 29.0 reduce-scatter.14
  325.7 30.2 reduce-scatter.16
  358.4 32.5 reduce-scatter.10
  393.2 33.7 reduce-scatter.20
  429.4 34.6 reduce-scatter.22
  466.8 28.8 reduce-scatter.24
  499.4 52.0 all-reduce.2
